TPU v7x, 256 devices: a whole 4x4x8 slice. The times are simulated.
256 devices in a mesh: seq: 32 (over x_hi, z, core), tensor: 8 (over x_lo, y).
Axes of the slice: x: 4 (x_hi: 2, x_lo: 2; x = x_hi * 2 + x_lo), y: 4, z: 8, core: 2. Of those that a mesh axis runs over, the one named last changes fastest.
Arguments:
- hidden: bfloat16 [8192, 2304], P('seq', 'tensor'), may hold values from -6 to 6
- attn_gain: float32 [2304], replicated, may hold values from 0.1 to 1.9
- query_weight: bfloat16 [2304, 2048], P(None, 'tensor'), may hold values from -1 to 1
- kv_weight: bfloat16 [2304, 2048], P(None, 'tensor'), may hold values from -1 to 1
- out_weight: bfloat16 [2048, 2304], P('tensor'), may hold values from -0.125 to 0.125
- post_gain: float32 [2304], replicated, may hold values from 0.1 to 1.9
- ff_gain: float32 [2304], replicated, may hold values from 0.1 to 1.9
- ff_post_gain: float32 [2304], replicated, may hold values from 0.1 to 1.9
- gate_weight: bfloat16 [2304, 9216], P('seq', 'tensor'), may hold values from -0.125 to 0.125
- up_weight: bfloat16 [2304, 9216], P('seq', 'tensor'), may hold values from -0.125 to 0.125
- down_weight_t: bfloat16 [2304, 9216], P('seq', 'tensor'), may hold values from -0.0625 to 0.0625
- next_gain: float32 [2304], replicated, may hold values from 0.1 to 1.9
- next_query_weight: bfloat16 [2304, 2048], P(None, 'tensor'), may hold values from -0.125 to 0.125
- next_kv_weight: bfloat16 [2304, 2048], P(None, 'tensor'), may hold values from -0.125 to 0.125
- lengths: int32 [4], replicated, may hold values from 256 to 3840, as said below
- pair_owner: int32 [32], replicated, may hold values from 0 to 31, each once
- page_table: int32 [64], replicated, may hold values from 0 to 63, each once
Outputs:
- hidden_out: bfloat16 [8192, 2304], P('seq', 'tensor')
- next_query: bfloat16 [8192, 2048], P('seq', 'tensor')
- next_kv: bfloat16 [8192, 2048], P('seq', 'tensor')
- kv_pages: bfloat16 [64, 128, 2048], P('seq', None, 'tensor')
Inputs may be any that keep to these rules, and one draw needn't show every extreme that they name: Four positive lengths summing to 8192; the first is the longest and the fourth the shortest. `pair_owner`: each mirrored pair b, the blocks b and 63 - b, is held by exactly one index of seq. `page_table`: every page takes exactly one block.
All inputs are finite; a program needn't handle non-finite values.
Results may differ from a plain program's by a relative error of at most 0.018.
Values may be sent and summed in bfloat16 or wider, within the bound.
A program may use at most 128 MiB of HBM per device.

v0:
```python
import jax
import jax.numpy as jnp
from jax import lax
from jax.sharding import PartitionSpec as P

EPS = 1e-06
SOFT_CAP = 50.0


def partner_2(block, axis, apart):
    count = lax.axis_size(axis)
    route = []
    for low in range(count):
        high = low | 1 << apart
        if high != low and high < count:
            route += [(low, high), (high, low)]
    return lax.ppermute(block, axis, route)


def row_norm(values, gain_vec):
    values = values.astype(jnp.float32)
    scale_vec = lax.rsqrt(jnp.mean(values * values, axis=-1, keepdims=True) + EPS)
    return values * scale_vec * gain_vec


def rotate(values, positions):
    half_dim = values.shape[-1] // 2
    freq_vec = 10000.0 ** (-jnp.arange(half_dim, dtype=jnp.float32) / half_dim)
    angles = positions.astype(jnp.float32)[:, None] * freq_vec[None, :]
    cosine_val = jnp.cos(angles)
    sine_val = jnp.sin(angles)
    leading = values[:, :half_dim]
    trailing = values[:, half_dim:]
    return jnp.concatenate(
        [leading * cosine_val - trailing * sine_val, trailing * cosine_val + leading * sine_val],
        axis=1,
    )


def tenant_of(stream_index, lengths):
    tenant_ends = jnp.cumsum(lengths)
    tenant_starts = tenant_ends - lengths
    tenant = jnp.sum((stream_index[:, None] >= tenant_ends[None, :3]).astype(jnp.int32), axis=1)
    selector = tenant[:, None] == jnp.arange(4, dtype=jnp.int32)[None, :]
    offset = jnp.sum(jnp.where(selector, tenant_starts[None, :], 0), axis=1)
    return (tenant, (stream_index - offset).astype(jnp.int32))


def body(
    hidden,
    attn_gain,
    query_weight,
    kv_weight,
    out_weight,
    post_gain,
    ff_gain,
    ff_post_gain,
    gate_weight,
    up_weight,
    down_weight_t,
    next_gain,
    next_query_weight,
    next_kv_weight,
    lengths,
    pair_owner,
    page_table,
):
    seq_count = lax.axis_size("seq")
    seq_index = lax.axis_index("seq")
    tensor_index = lax.axis_index("tensor")
    rows = hidden.shape[0]
    rows_half = rows // 2
    share = hidden.shape[1]
    head_dim = query_weight.shape[1]
    is_key = tensor_index % 2 == 0
    owned_pair = jnp.sum(
        jnp.where(jnp.arange(seq_count, dtype=jnp.int32) == seq_index, pair_owner, 0)
    )
    local_range = jnp.arange(rows_half, dtype=jnp.int32)
    tags = jnp.concatenate(
        [
            owned_pair * rows_half + local_range,
            (2 * seq_count - 1 - owned_pair) * rows_half + local_range,
        ]
    )
    tenant, position = tenant_of(tags, lengths)
    block_ids = jnp.arange(2 * seq_count, dtype=jnp.int32)
    page_blocks = [
        jnp.sum(jnp.where(page_table == 2 * seq_index + slot_index, block_ids, 0))
        for slot_index in range(2)
    ]
    wanted_tags = jnp.concatenate(
        [page_blocks[0] * rows_half + local_range, page_blocks[1] * rows_half + local_range]
    )
    full_hidden = lax.all_gather(hidden, "tensor", axis=1, tiled=True)
    attn_input = row_norm(full_hidden, attn_gain).astype(jnp.bfloat16)
    queries = rotate(
        jnp.dot(attn_input, query_weight, preferred_element_type=jnp.float32), position
    ).astype(jnp.bfloat16)
    own_proj = jnp.dot(attn_input, kv_weight, preferred_element_type=jnp.float32)
    own_part = jnp.where(is_key, rotate(own_proj, position), own_proj).astype(jnp.bfloat16)
    query_scale = head_dim ** (-0.5)
    partner = partner_2(own_part, "tensor", 0)
    key_mine = jnp.where(is_key, own_part, partner)
    value_mine = jnp.where(is_key, partner, own_part)
    key_rows = lax.all_gather(key_mine, "seq", axis=0, tiled=True)
    value_rows = lax.all_gather(value_mine, "seq", axis=0, tiled=True)
    key_tags = lax.all_gather(tags, "seq", axis=0, tiled=True)
    key_tenant, key_position = tenant_of(key_tags, lengths)
    allowed = (tenant[:, None] == key_tenant[None, :]) & (key_tags[None, :] <= tags[:, None])
    raw_scores = (
        lax.dot_general(
            queries, key_rows, (((1,), (1,)), ((), ())), preferred_element_type=jnp.float32
        )
        * query_scale
    )
    capped = SOFT_CAP * jnp.tanh(raw_scores / SOFT_CAP)
    weights = jnp.where(allowed, jnp.exp(capped), 0.0).astype(jnp.bfloat16)
    own_rows = jnp.where(is_key, key_rows, value_rows)
    numerator = jnp.dot(weights, value_rows, preferred_element_type=jnp.float32)
    denominator = jnp.sum(weights.astype(jnp.float32), axis=1)
    picker = (wanted_tags[:, None] == key_tags[None, :]).astype(jnp.bfloat16)
    cache_acc = jnp.dot(picker, own_rows, preferred_element_type=jnp.float32)
    attended = (numerator / denominator[:, None]).astype(jnp.bfloat16)
    attn_partial = jnp.dot(attended, out_weight, preferred_element_type=jnp.float32)
    column_start = tensor_index * share
    attn_sum = lax.psum(attn_partial, "tensor")
    middle = (full_hidden.astype(jnp.float32) + row_norm(attn_sum, post_gain)).astype(jnp.bfloat16)
    ff_input = row_norm(middle, ff_gain).astype(jnp.bfloat16)
    gate_val = jnp.dot(
        ff_input,
        lax.all_gather(gate_weight, "seq", axis=0, tiled=True),
        preferred_element_type=jnp.float32,
    )
    up_val = jnp.dot(
        ff_input,
        lax.all_gather(up_weight, "seq", axis=0, tiled=True),
        preferred_element_type=jnp.float32,
    )
    inner = (jax.nn.gelu(gate_val, approximate=True) * up_val).astype(jnp.bfloat16)
    ff_partial = lax.dot_general(
        inner,
        lax.all_gather(down_weight_t, "seq", axis=0, tiled=True),
        (((1,), (1,)), ((), ())),
        preferred_element_type=jnp.float32,
    )
    ff_sum = lax.psum(ff_partial.astype(jnp.bfloat16), "tensor").astype(jnp.float32)
    final_rows = (middle.astype(jnp.float32) + row_norm(ff_sum, ff_post_gain)).astype(jnp.bfloat16)
    next_input = row_norm(final_rows, next_gain).astype(jnp.bfloat16)
    hidden_out = lax.dynamic_slice_in_dim(final_rows, column_start, share, 1)
    next_query = rotate(
        jnp.dot(next_input, next_query_weight, preferred_element_type=jnp.float32), position
    ).astype(jnp.bfloat16)
    next_proj = jnp.dot(next_input, next_kv_weight, preferred_element_type=jnp.float32)
    next_kv = jnp.where(is_key, rotate(next_proj, position), next_proj).astype(jnp.bfloat16)
    kv_pages = cache_acc.astype(jnp.bfloat16).reshape(2, rows_half, head_dim)
    return (hidden_out, next_query, next_kv, kv_pages)


def solution(mesh):
    in_specs = (
        P("seq", "tensor"),
        P(),
        P(None, "tensor"),
        P(None, "tensor"),
        P("tensor", None),
        P(),
        P(),
        P(),
        P("seq", "tensor"),
        P("seq", "tensor"),
        P("seq", "tensor"),
        P(),
        P(None, "tensor"),
        P(None, "tensor"),
        P(),
        P(),
        P(),
    )
    out_specs = (
        P("seq", "tensor"),
        P("seq", "tensor"),
        P("seq", "tensor"),
        P("seq", None, "tensor"),
    )
    return jax.shard_map(body, mesh=mesh, in_specs=in_specs, out_specs=out_specs, check_vma=False)
```

profile of v0, /device:TPU:4, one launch (start us, length us, event | category | flops | bytes accessed | tf_op | source)
XLA Modules:
  0.0 710.7 jit_solution(15065292437494655086)
XLA Ops:
  7.2 0.7 all-gather.8.cloned.1.call-update
  8.0 1.3 fusion.89
  10.6 0.8 reduce-window.4
  11.5 0.7 bitcast_subtract_fusion
  12.2 0.1 select_reduce_fusion
  12.3 41.9 %all-gather.8.cloned.1.call-done = bf16[256,2304]{0,1:T(8,128)(2,1)} async-done(((bf16[256,288]{0,1:T(8,128)(2,1)}), bf16[256,2304]{0,1:T(8,128)(2,1)}) %all-gather.8.cloned.1.call-update) | async-done | bytes 1179664 | tf_op jit(solution)/shard_map/all_gather | solution.py:95
  54.2 1.6 copy.29
  55.8 0.3 fusion.17
  56.1 2.0 fusion.47
  58.2 0.6 fusion.77
  58.8 0.1 collective-permute-start
  58.9 5.0 collective-permute-done
  63.8 0.7 broadcast_select_fusion
  64.6 0.7 all-gather.12.cloned.1.call-update
  65.4 40.0 %all-gather = s32[32,1,256]{2,1,0:T(1,128)S(1)} all-gather(s32[1,1,256]{2,1,0:T(1,128)S(1)} %bitcast.22), channel_id=1, replica_groups=mesh['seq'=32,'tensor'=8] {'seq'}, dimensions={0}, use_global_device_ids=true | all-gather | bytes 33792 | tf_op jit(solution)/shard_map/all_gather | solution.py:108
  105.4 0.2 convert_reduce_fusion.1
  105.5 2.0 fusion.49
  107.6 0.6 fusion.74
  108.1 40.5 %all-gather.10.cloned.1.call-done = bf16[8192,256]{0,1:T(8,128)(2,1)} async-done(((bf16[256,256]{0,1:T(8,128)(2,1)}), bf16[8192,256]{0,1:T(8,128)(2,1)}) %all-gather.10.cloned.1.call-update) | async-done | bytes 4194320 | tf_op jit(solution)/shard_map/all_gather | solution.py:106
  148.7 7.5 %convert_reduce_fusion = (f32[256]{0:T(256)S(1)}, bf16[256,8192]{1,0:T(8,128)(2,1)}) fusion(bf16[8192,256]{0,1:T(8,128)(2,1)} %all-gather.10.cloned.1.call-done, bf16[256,128]{0,1:T(8,128)(2,1)S(1)} %get-tuple-element.27, bf16[256,128]{0,1:T(8,128)(2,1)S(1)} %get-tuple-element.26, s32[256]{0:T(256)S(1)} %pad_add_fusion, s32[8192]{0:T(1024)S(1)} %bitcast.20, ...), kind=kOutput, calls=%fused_computation.6 | convolution fusion | flops 1092878080 | bytes 8588288 | tf_op jit(solution)/shard_map/dot_general | solution.py:112
  156.1 79.5 %all-gather.12.cloned.1.call-done = bf16[8192,256]{0,1:T(8,128)(2,1)} async-done(((bf16[256,256]{0,1:T(8,128)(2,1)}), bf16[8192,256]{0,1:T(8,128)(2,1)}) %all-gather.12.cloned.1.call-update) | async-done | bytes 4194320 | tf_op jit(solution)/shard_map/all_gather | solution.py:107
  235.6 7.2 %fusion.38 = f32[256,2304]{1,0:T(8,128)} fusion(bf16[256,2304]{1,0:T(8,128)(2,1)S(1)} %copy-done, bf16[256,8192]{1,0:T(8,128)(2,1)} %get-tuple-element.33, bf16[8192,256]{0,1:T(8,128)(2,1)} %all-gather.12.cloned.1.call-done, f32[256]{0:T(256)S(1)} %get-tuple-element.32), kind=kOutput, calls=%fused_computation.51 | convolution fusion | flops 1375862784 | bytes 11928576 | tf_op jit(solution)/shard_map/dot_general | solution.py:125
  242.9 0.5 all-gather.14.cloned.1.call-update
  243.5 0.5 all-gather.16.cloned.1.call-update
  244.1 0.7 all-gather.18.cloned.1.call-update
  244.8 0.2 all-reduce.5.cloned.1.call-start
  245.0 86.2 %all-reduce.3.cloned.1.call-done = f32[256,2304]{1,0:T(8,128)} async-done(((f32[256,2304]{1,0:T(8,128)}), f32[256,2304]{1,0:T(8,128)}) %all-reduce.3.cloned.1.call-update) | async-done | bytes 2359312 | tf_op jit(solution)/shard_map/psum | solution.py:127
  331.2 2.1 multiply_reduce_fusion
  333.3 0.3 copy-done.1
  333.6 0.7 fusion.21
  334.3 88.3 %all-gather.14.cloned.1.call-done = bf16[2304,1152]{1,0:T(8,128)(2,1)} async-done(((bf16[72,1152]{1,0:T(8,128)(2,1)}), bf16[2304,1152]{1,0:T(8,128)(2,1)}) %all-gather.14.cloned.1.call-update) | async-done | bytes 5308432 | tf_op jit(solution)/shard_map/all_gather | solution.py:132
  422.6 5.4 fusion.45
  427.9 84.7 %all-gather.16.cloned.1.call-done = bf16[2304,1152]{1,0:T(8,128)(2,1)} async-done(((bf16[72,1152]{1,0:T(8,128)(2,1)}), bf16[2304,1152]{1,0:T(8,128)(2,1)}) %all-gather.16.cloned.1.call-update) | async-done | bytes 5308432 | tf_op jit(solution)/shard_map/all_gather | solution.py:137
  512.7 90.3 %all-gather.18.cloned.1.call-done = bf16[2304,1152]{1,0:T(8,128)(2,1)} async-done(((bf16[72,1152]{1,0:T(8,128)(2,1)}), bf16[2304,1152]{1,0:T(8,128)(2,1)}) %all-gather.18.cloned.1.call-update) | async-done | bytes 5308432 | tf_op jit(solution)/shard_map/all_gather | solution.py:143
  602.9 8.8 %convolution_convert_fusion = bf16[256,2304]{1,0:T(8,128)(2,1)} fusion(bf16[2304,1152]{1,0:T(8,128)(2,1)} %all-gather.18.cloned.1.call-done, bf16[2304,1152]{1,0:T(8,128)(2,1)} %all-gather.16.cloned.1.call-done, f32[256,1152]{1,0:T(8,128)} %fusion.45, bf16[256,2304]{1,0:T(8,128)(2,1)S(1)} %get-tuple-element.21, f32[2304]{0:T(1024)S(1)} %copy-done.11, ...), kind=kOutput, calls=%fused_computation.13 | convolution fusion | flops 2723807232 | bytes 14166016 | tf_op jit(solution)/shard_map/dot_general | solution.py:141
  611.8 0.6 fusion.90
  613.8 4.4 fusion.32
  618.2 75.5 %all-reduce.5.cloned.1.call-done = bf16[256,2304]{1,0:T(8,128)(2,1)} async-done(((bf16[256,2304]{1,0:T(8,128)(2,1)}), bf16[256,2304]{1,0:T(8,128)(2,1)}) %all-reduce.5.cloned.1.call-update) | async-done | bytes 1179664 | tf_op jit(solution)/shard_map/psum | solution.py:147
  693.7 1.7 fusion.12
  695.4 2.0 fusion.14
  697.4 0.7 fusion.51
  698.2 0.6 fusion.83
  698.8 0.8 copy.32
  699.6 2.0 fusion.53
  701.6 0.6 fusion.80
  702.2 0.8 copy.31
  702.9 0.1 constant_dynamic-slice_fusion
  703.1 0.8 copy.30
  (53 shorter events, 0.6 us)
Async XLA Ops:
  7.2 228.4 %copy-start = (bf16[256,2304]{1,0:T(8,128)(2,1)S(1)}, bf16[256,2304]{1,0:T(8,128)(2,1)}, u32[]{:S(2)}) copy-start(bf16[256,2304]{1,0:T(8,128)(2,1)} %param.21) | copy-start | bytes 3538948
  7.2 49.0 %copy-start.10 = (f32[2304]{0:T(1024)S(1)}, f32[2304]{0:T(1024)}, u32[]{:S(2)}) copy-start(f32[2304]{0:T(1024)} %param.18) | copy-start | bytes 27652
  7.2 47.0 %all-gather.8.cloned.1.call-start = ((), (), s32[]{:S(2)}) async-start(), calls=%async_computation | async-start | bytes 1327104 | tf_op jit(solution)/shard_map/all_gather | solution.py:95
  7.9 140.7 %all-gather.10.cloned.1.call-start = ((), (), s32[]{:S(2)}) async-start(), calls=%async_computation.1 | async-start | bytes 4325376 | tf_op jit(solution)/shard_map/all_gather | solution.py:106
  11.4 96.1 %copy-start.6 = (f32[128]{0:T(128)}, f32[128]{0:T(128)S(1)}, u32[]{:S(2)}) copy-start(f32[128]{0:T(128)S(1)} %multiply_power_fusion) | copy-start | bytes 1540
  58.8 5.1 collective-permute-start
  64.6 171.0 %all-gather.12.cloned.1.call-start = ((), (), s32[]{:S(2)}) async-start(), calls=%async_computation.2 | async-start | bytes 4325376 | tf_op jit(solution)/shard_map/all_gather | solution.py:107
  65.3 265.9 %all-reduce.3.cloned.1.call-start = ((), (), s32[]{:S(2)}) async-start(), calls=%async_computation.3 | async-start | bytes 4718592 | tf_op jit(solution)/shard_map/psum | solution.py:127
  105.4 50.8 %copy-start.2 = (s32[32,1,256]{2,1,0:T(1,128)}, s32[32,1,256]{2,1,0:T(1,128)S(1)}, u32[]{:S(2)}) copy-start(s32[32,1,256]{2,1,0:T(1,128)S(1)} %all-gather) | copy-start | bytes 98308
  242.8 90.4 %copy-start.4 = (f32[2304]{0:T(1024)S(1)}, f32[2304]{0:T(1024)}, u32[]{:S(2)}) copy-start(f32[2304]{0:T(1024)} %param.22) | copy-start | bytes 27652
  242.9 179.7 %all-gather.14.cloned.1.call-start = ((), (), s32[]{:S(2)}) async-start(), calls=%async_computation.4 | async-start | bytes 5474304 | tf_op jit(solution)/shard_map/all_gather | solution.py:132
  243.5 269.2 %all-gather.16.cloned.1.call-start = ((), (), s32[]{:S(2)}) async-start(), calls=%async_computation.5 | async-start | bytes 5474304 | tf_op jit(solution)/shard_map/all_gather | solution.py:137
  244.0 358.9 %all-gather.18.cloned.1.call-start = ((), (), s32[]{:S(2)}) async-start(), calls=%async_computation.6 | async-start | bytes 5474304 | tf_op jit(solution)/shard_map/all_gather | solution.py:143
  244.8 448.9 %all-reduce.5.cloned.1.call-start = ((), (), s32[]{:S(2)}) async-start(), calls=%async_computation.7 | async-start | bytes 2359296 | tf_op jit(solution)/shard_map/psum | solution.py:147
  331.2 2.4 copy-start.1
  422.6 180.4 %copy-start.11 = (f32[2304]{0:T(1024)S(1)}, f32[2304]{0:T(1024)}, u32[]{:S(2)}) copy-start(f32[2304]{0:T(1024)} %param.23) | copy-start | bytes 27652
  427.9 183.9 %copy-start.8 = (s32[64]{0:T(128)S(1)}, s32[64]{0:T(128)}, u32[]{:S(2)}) copy-start(s32[64]{0:T(128)} %param.33) | copy-start | bytes 772
  427.9 185.8 %copy-start.3 = (s32[32,1,256]{2,1,0:T(1,128)S(1)}, s32[32,1,256]{2,1,0:T(1,128)}, u32[]{:S(2)}) copy-start(s32[32,1,256]{2,1,0:T(1,128)} %copy-done.2) | copy-start | bytes 98308
  613.8 81.6 %copy-start.5 = (f32[2304]{0:T(1024)S(1)}, f32[2304]{0:T(1024)}, u32[]{:S(2)}) copy-start(f32[2304]{0:T(1024)} %param.24) | copy-start | bytes 27652
  693.7 3.7 copy-start.9
  693.7 3.7 copy-start.12
  697.4 0.8 copy-start.7
  697.4 2.2 copy-start.13
Sparse Core Ops, SparseCore 0:
  9.8 44.3 all-gather.7
  64.7 83.9 all-gather.9
  151.8 83.7 all-gather.11
  243.0 88.1 all-reduce.2
  333.7 88.7 all-gather.13
  425.1 87.5 all-gather.15
  515.4 87.5 all-gather.17
  611.9 81.7 all-reduce.4
where the time goes:
time: 711 us
  waiting for transfers between devices  595 us (84%)
  matrix products  40.1 us (6%)
  blocking collectives  40 us (6%)
  between operations  17 us (2%)
  other arithmetic  13.6 us (2%)
    all_gather x1, waiting for transfers between devices, body(): lax.all_gather(down_weight_t, 'seq', axis=0, tiled=True)  90.3 us
    all_gather x1, waiting for transfers between devices, body(): lax.all_gather(gate_weight, 'seq', axis=0, tiled=True)  88.3 us
    psum x1, waiting for transfers between devices, body(): attn_sum = lax.psum(attn_partial, 'tensor')  86.2 us
    all_gather x1, waiting for transfers between devices, body(): lax.all_gather(up_weight, 'seq', axis=0, tiled=True)  84.7 us
    all_gather x1, waiting for transfers between devices, body(): value_rows = lax.all_gather(value_mine, 'seq', axis=0, tiled=True)  79.5 us
    psum x1, waiting for transfers between devices, body(): lax.psum(ff_partial.astype(jnp.bfloat16), 'tensor').astype(jnp.float32)  75.5 us
    all_gather x1, waiting for transfers between devices, body(): full_hidden = lax.all_gather(hidden, 'tensor', axis=1, tiled=True)  41.9 us
    all_gather x1, waiting for transfers between devices, body(): key_rows = lax.all_gather(key_mine, 'seq', axis=0, tiled=True)  40.5 us
  transfers between devices with their start and end apart: 9, of which 9 were waited for; matrix products, arithmetic and copies ran while one was open for 4% of the time, Pallas kernels for 0%

commit v1 on v0

--- a/solution.py
+++ b/solution.py
@@ -134,7 +134,9 @@
     )
     up_val = jnp.dot(
         ff_input,
-        lax.all_gather(up_weight, "seq", axis=0, tiled=True),
+        jnp.concatenate(
+            lax.all_to_all(jnp.stack([up_weight] * lax.axis_size("seq")), "seq", 0, 0), axis=0
+        ),
         preferred_element_type=jnp.float32,
     )
     inner = (jax.nn.gelu(gate_val, approximate=True) * up_val).astype(jnp.bfloat16)

time: 711 us -> 659 us (0.927)
  waiting for transfers between devices: 595 us -> 532 us
  starting transfers between devices: 0.58 us -> 8.09 us
    all_gather x1 -> x0, waiting for transfers between devices: 84.7 us -> none  [body(): lax.all_gather(up_weight, 'seq', axis=0, tiled=True)]
    psum x1, waiting for transfers between devices: 86.2 us -> 112 us  [body(): attn_sum = lax.psum(attn_partial, 'tensor')]
    all_to_all x0 -> x1, starting transfers between devices: none -> 7.54 us  [body(): lax.all_to_all(jnp.stack([up_weight] * lax.axis_size('seq')), 'seq', 0, 0)]
  transfers between devices with their start and end apart: 9 -> 9, of which waited for: 9 -> 8; matrix products, arithmetic and copies ran while one was open for 4% -> 4% of each run, Pallas kernels for 0% -> 0%
where the time goes in v1:
time: 659 us; the launch traced here: 658 us
  waiting for transfers between devices  532 us (81%)
  matrix products  40 us (6%)
  blocking collectives  40 us (6%)
  between operations  17 us (3%)
  other arithmetic  13.6 us (2%)
  starting transfers between devices  8.09 us (1%)
  local copies, waits for them, and re-layouts  7.31 us (1%)
    psum x1, waiting for transfers between devices, body(): attn_sum = lax.psum(attn_partial, 'tensor')  112 us
    all_gather x1, waiting for transfers between devices, body(): lax.all_gather(gate_weight, 'seq', axis=0, tiled=True)  90.3 us
    all_gather x1, waiting for transfers between devices, body(): lax.all_gather(down_weight_t, 'seq', axis=0, tiled=True)  84.8 us
    all_gather x1, waiting for transfers between devices, body(): value_rows = lax.all_gather(value_mine, 'seq', axis=0, tiled=True)  79.5 us
    psum x1, waiting for transfers between devices, body(): lax.psum(ff_partial.astype(jnp.bfloat16), 'tensor').astype(jnp.float32)  75.5 us
    all_gather x1, waiting for transfers between devices, body(): full_hidden = lax.all_gather(hidden, 'tensor', axis=1, tiled=True)  41.9 us
    all_gather x1, waiting for transfers between devices, body(): key_rows = lax.all_gather(key_mine, 'seq', axis=0, tiled=True)  40.5 us
    all_gather x1, blocking collectives, body(): key_tags = lax.all_gather(tags, 'seq', axis=0, tiled=True)  40 us
  transfers between devices with their start and end apart: 9, of which 8 were waited for; matrix products, arithmetic and copies ran while one was open for 4% of the time, Pallas kernels for 0%

profile of v1, /device:TPU:4, one launch (start us, length us, event | category | flops | bytes accessed | tf_op | source)
XLA Modules:
  0.0 658.0 jit_solution(14095452790835733)
XLA Ops:
  7.2 0.7 all-gather.7.cloned.1.call-update
  8.0 1.3 fusion.89
  10.6 0.8 reduce-window.4
  11.5 0.7 bitcast_subtract_fusion
  12.3 41.9 %all-gather.7.cloned.1.call-done = bf16[256,2304]{0,1:T(8,128)(2,1)} async-done(((bf16[256,288]{0,1:T(8,128)(2,1)}), bf16[256,2304]{0,1:T(8,128)(2,1)}) %all-gather.7.cloned.1.call-update) | async-done | bytes 1179664 | tf_op jit(solution)/shard_map/all_gather | solution.py:95
  54.2 1.6 copy.29
  55.8 0.3 fusion.17
  56.1 2.0 fusion.47
  58.2 0.6 fusion.77
  58.8 0.1 collective-permute-start
  58.9 5.0 collective-permute-done
  63.8 0.7 broadcast_select_fusion
  64.6 0.7 all-gather.11.cloned.1.call-update
  65.4 40.0 %all-gather = s32[32,1,256]{2,1,0:T(1,128)S(1)} all-gather(s32[1,1,256]{2,1,0:T(1,128)S(1)} %bitcast.23), channel_id=1, replica_groups=mesh['seq'=32,'tensor'=8] {'seq'}, dimensions={0}, use_global_device_ids=true | all-gather | bytes 33792 | tf_op jit(solution)/shard_map/all_gather | solution.py:108
  105.4 0.2 convert_reduce_fusion.1
  105.5 2.0 fusion.49
  107.6 0.6 fusion.74
  108.1 40.5 %all-gather.9.cloned.1.call-done = bf16[8192,256]{0,1:T(8,128)(2,1)} async-done(((bf16[256,256]{0,1:T(8,128)(2,1)}), bf16[8192,256]{0,1:T(8,128)(2,1)}) %all-gather.9.cloned.1.call-update) | async-done | bytes 4194320 | tf_op jit(solution)/shard_map/all_gather | solution.py:106
  148.7 7.5 %convert_reduce_fusion = (f32[256]{0:T(256)S(1)}, bf16[256,8192]{1,0:T(8,128)(2,1)}) fusion(bf16[8192,256]{0,1:T(8,128)(2,1)} %all-gather.9.cloned.1.call-done, bf16[256,128]{0,1:T(8,128)(2,1)S(1)} %get-tuple-element.27, bf16[256,128]{0,1:T(8,128)(2,1)S(1)} %get-tuple-element.26, s32[256]{0:T(256)S(1)} %pad_add_fusion, s32[8192]{0:T(1024)S(1)} %bitcast.21, ...), kind=kOutput, calls=%fused_computation.6 | convolution fusion | flops 1092878080 | bytes 8588288 | tf_op jit(solution)/shard_map/dot_general | solution.py:112
  156.1 79.5 %all-gather.11.cloned.1.call-done = bf16[8192,256]{0,1:T(8,128)(2,1)} async-done(((bf16[256,256]{0,1:T(8,128)(2,1)}), bf16[8192,256]{0,1:T(8,128)(2,1)}) %all-gather.11.cloned.1.call-update) | async-done | bytes 4194320 | tf_op jit(solution)/shard_map/all_gather | solution.py:107
  235.6 7.2 %fusion.38 = f32[256,2304]{1,0:T(8,128)} fusion(bf16[256,2304]{1,0:T(8,128)(2,1)S(1)} %copy-done, bf16[256,8192]{1,0:T(8,128)(2,1)} %get-tuple-element.33, bf16[8192,256]{0,1:T(8,128)(2,1)} %all-gather.11.cloned.1.call-done, f32[256]{0:T(256)S(1)} %get-tuple-element.32), kind=kOutput, calls=%fused_computation.51 | convolution fusion | flops 1375862784 | bytes 11928576 | tf_op jit(solution)/shard_map/dot_general | solution.py:125
  242.8 0.5 all-gather.13.cloned.1.call-update
  243.4 0.3 copy-done.2
  243.7 2.6 stack.2
  246.3 7.5 %all-to-all-start = ((bf16[32,72,1152]{2,1,0:T(8,128)(2,1)}), bf16[32,72,1152]{2,1,0:T(8,128)(2,1)}, u32[]{:S(2)}, u32[]{:S(2)}) async-start(bf16[32,72,1152]{2,1,0:T(8,128)(2,1)} %stack.2), calls=%async_computation | async-start | bytes 10616832 | tf_op jit(solution)/shard_map/all_to_all | solution.py:138
  253.9 0.5 all-gather.15.cloned.1.call-update
  254.5 0.2 all-reduce.5.cloned.1.call-start
  254.7 112.0 %all-reduce.3.cloned.1.call-done = f32[256,2304]{1,0:T(8,128)} async-done(((f32[256,2304]{1,0:T(8,128)}), f32[256,2304]{1,0:T(8,128)}) %all-reduce.3.cloned.1.call-update) | async-done | bytes 2359312 | tf_op jit(solution)/shard_map/psum | solution.py:127
  366.7 2.1 multiply_reduce_fusion
  368.8 0.3 copy-done.1
  369.1 0.7 fusion.21
  369.7 90.3 %all-gather.13.cloned.1.call-done = bf16[2304,1152]{1,0:T(8,128)(2,1)} async-done(((bf16[72,1152]{1,0:T(8,128)(2,1)}), bf16[2304,1152]{1,0:T(8,128)(2,1)}) %all-gather.13.cloned.1.call-update) | async-done | bytes 5308432 | tf_op jit(solution)/shard_map/all_gather | solution.py:132
  460.1 5.3 fusion.45
  465.4 84.8 %all-gather.15.cloned.1.call-done = bf16[2304,1152]{1,0:T(8,128)(2,1)} async-done(((bf16[72,1152]{1,0:T(8,128)(2,1)}), bf16[2304,1152]{1,0:T(8,128)(2,1)}) %all-gather.15.cloned.1.call-update) | async-done | bytes 5308432 | tf_op jit(solution)/shard_map/all_gather | solution.py:145
  550.2 8.9 %convolution_convert_fusion = bf16[256,2304]{1,0:T(8,128)(2,1)} fusion(bf16[2304,1152]{1,0:T(8,128)(2,1)} %all-gather.15.cloned.1.call-done, bf16[2304,1152]{1,0:T(8,128)(2,1)} %bitcast.5, f32[256,1152]{1,0:T(8,128)} %fusion.45, bf16[256,2304]{1,0:T(8,128)(2,1)S(1)} %get-tuple-element.21, f32[2304]{0:T(1024)S(1)} %copy-done.12, f32[256]{0:T(256)S(1)} %add_rsqrt_fusion.2), kind=kOutput, calls=%fused_computation.13 | convolution fusion | flops 2723807232 | bytes 14166016 | tf_op jit(solution)/shard_map/dot_general | solution.py:143
  559.1 0.6 fusion.90
  561.1 4.4 fusion.32
  565.5 75.5 %all-reduce.5.cloned.1.call-done = bf16[256,2304]{1,0:T(8,128)(2,1)} async-done(((bf16[256,2304]{1,0:T(8,128)(2,1)}), bf16[256,2304]{1,0:T(8,128)(2,1)}) %all-reduce.5.cloned.1.call-update) | async-done | bytes 1179664 | tf_op jit(solution)/shard_map/psum | solution.py:149
  641.0 1.7 fusion.12
  642.7 2.0 fusion.14
  644.8 0.7 fusion.51
  645.5 0.6 fusion.83
  646.1 0.8 copy.32
  646.9 2.0 fusion.53
  648.9 0.6 fusion.80
  649.5 0.8 copy.31
  650.2 0.1 constant_dynamic-slice_fusion
  650.4 0.8 copy.30
  (55 shorter events, 0.7 us)
Async XLA Ops:
  7.2 228.4 %copy-start = (bf16[256,2304]{1,0:T(8,128)(2,1)S(1)}, bf16[256,2304]{1,0:T(8,128)(2,1)}, u32[]{:S(2)}) copy-start(bf16[256,2304]{1,0:T(8,128)(2,1)} %param.21) | copy-start | bytes 3538948
  7.2 49.0 %copy-start.11 = (f32[2304]{0:T(1024)S(1)}, f32[2304]{0:T(1024)}, u32[]{:S(2)}) copy-start(f32[2304]{0:T(1024)} %param.18) | copy-start | bytes 27652
  7.2 47.0 %all-gather.7.cloned.1.call-start = ((), (), s32[]{:S(2)}) async-start(), calls=%async_computation.1 | async-start | bytes 1327104 | tf_op jit(solution)/shard_map/all_gather | solution.py:95
  7.9 140.7 %all-gather.9.cloned.1.call-start = ((), (), s32[]{:S(2)}) async-start(), calls=%async_computation.2 | async-start | bytes 4325376 | tf_op jit(solution)/shard_map/all_gather | solution.py:106
  11.4 96.1 %copy-start.7 = (f32[128]{0:T(128)}, f32[128]{0:T(128)S(1)}, u32[]{:S(2)}) copy-start(f32[128]{0:T(128)S(1)} %multiply_power_fusion) | copy-start | bytes 1540
  58.8 5.1 collective-permute-start
  64.6 171.0 %all-gather.11.cloned.1.call-start = ((), (), s32[]{:S(2)}) async-start(), calls=%async_computation.3 | async-start | bytes 4325376 | tf_op jit(solution)/shard_map/all_gather | solution.py:107
  65.3 301.4 %all-reduce.3.cloned.1.call-start = ((), (), s32[]{:S(2)}) async-start(), calls=%async_computation.4 | async-start | bytes 4718592 | tf_op jit(solution)/shard_map/psum | solution.py:127
  105.4 50.8 %copy-start.3 = (s32[32,1,256]{2,1,0:T(1,128)}, s32[32,1,256]{2,1,0:T(1,128)S(1)}, u32[]{:S(2)}) copy-start(s32[32,1,256]{2,1,0:T(1,128)S(1)} %all-gather) | copy-start | bytes 98308
  242.8 0.9 copy-start.2
  242.8 217.3 %all-gather.13.cloned.1.call-start = ((), (), s32[]{:S(2)}) async-start(), calls=%async_computation.5 | async-start | bytes 5474304 | tf_op jit(solution)/shard_map/all_gather | solution.py:132
  246.3 219.1 %all-to-all-start = ((bf16[32,72,1152]{2,1,0:T(8,128)(2,1)}), bf16[32,72,1152]{2,1,0:T(8,128)(2,1)}, u32[]{:S(2)}, u32[]{:S(2)}) async-start(bf16[32,72,1152]{2,1,0:T(8,128)(2,1)} %stack.2), calls=%async_computation | async-start | bytes 10616832 | tf_op jit(solution)/shard_map/all_to_all | solution.py:138
  253.9 114.9 %copy-start.5 = (f32[2304]{0:T(1024)S(1)}, f32[2304]{0:T(1024)}, u32[]{:S(2)}) copy-start(f32[2304]{0:T(1024)} %param.22) | copy-start | bytes 27652
  253.9 296.3 %all-gather.15.cloned.1.call-start = ((), (), s32[]{:S(2)}) async-start(), calls=%async_computation.6 | async-start | bytes 5474304 | tf_op jit(solution)/shard_map/all_gather | solution.py:145
  254.5 386.5 %all-reduce.5.cloned.1.call-start = ((), (), s32[]{:S(2)}) async-start(), calls=%async_computation.7 | async-start | bytes 2359296 | tf_op jit(solution)/shard_map/psum | solution.py:149
  366.7 2.4 copy-start.1
  460.1 90.1 %copy-start.12 = (f32[2304]{0:T(1024)S(1)}, f32[2304]{0:T(1024)}, u32[]{:S(2)}) copy-start(f32[2304]{0:T(1024)} %param.23) | copy-start | bytes 27652
  550.2 8.9 %copy-start.9 = (s32[64]{0:T(128)S(1)}, s32[64]{0:T(128)}, u32[]{:S(2)}) copy-start(s32[64]{0:T(128)} %param.33) | copy-start | bytes 772
  550.2 10.9 %copy-start.4 = (s32[32,1,256]{2,1,0:T(1,128)S(1)}, s32[32,1,256]{2,1,0:T(1,128)}, u32[]{:S(2)}) copy-start(s32[32,1,256]{2,1,0:T(1,128)} %copy-done.3) | copy-start | bytes 98308
  561.1 81.6 %copy-start.6 = (f32[2304]{0:T(1024)S(1)}, f32[2304]{0:T(1024)}, u32[]{:S(2)}) copy-start(f32[2304]{0:T(1024)} %param.24) | copy-start | bytes 27652
  641.0 3.7 copy-start.10
  641.0 3.7 copy-start.13
  644.7 0.8 copy-start.8
  644.7 2.2 copy-start.14
Sparse Core Ops, SparseCore 0:
  9.8 44.3 all-gather.6
  64.7 83.9 all-gather.8
  151.8 83.7 all-gather.10
  242.9 123.7 all-reduce.2
  369.2 90.8 all-gather.12
  462.6 87.5 all-gather.14
  559.2 81.7 all-reduce.4
